TPU v7x, 128 devices: a whole 4x4x4 slice. The times are simulated.
128 devices in a mesh: band: 16 (over z, x), rows: 8 (over y, core).
Axes of the slice: x: 4, y: 4, z: 4, core: 2. Of those that a mesh axis runs over, the one named last changes fastest.
Arguments:
- latents: bfloat16 [107520, 16], P(('band', 'rows')), may hold values from -6 to 6
- token_cell: int32 [107520], P(('band', 'rows')), may hold values from 0 to 107519, as said below
- frame_counts: int32 [16], replicated, may hold values from 1 to 4, 21 in all
- in_kernel: bfloat16 [3, 3, 3, 16, 384], replicated, may hold values from -0.3125 to 0.3125
- in_bias: float32 [384], replicated, may hold values from -3 to 3
- mid_kernel: bfloat16 [3, 3, 3, 384, 384], replicated, may hold values from -0.0625 to 0.0625
- mid_bias: float32 [384], replicated, may hold values from -3 to 3
Outputs:
- decoded: bfloat16 [64, 32, 160, 384], P('band', 'rows')
Inputs may be any that keep to these rules, and one draw needn't show every extreme that they name: `token_cell`: rows d * 840 to (d + 1) * 840 - 1 (d the flat index over band+rows) are, in some order, the cells f * 32 * 160 + d * 40 + s for every f < 21 and s < 40, each once. `frame_counts`: the counts sum to 21; some band holds 4 frames.
All inputs are finite; a program needn't handle non-finite values.
Results may differ from a plain program's by a relative error of at most 0.0043.
Values may be sent and summed in bfloat16 or wider, within the bound.
No kernel may reach another device: no remote copies, remote signals or barrier semaphores. Data moves between devices by JAX's collectives and lax.ppermute only.
A program may use at most 64 MiB of HBM per device.

v0:
```python
import jax
import jax.numpy as jnp
from jax import lax
from jax.sharding import PartitionSpec as P

W = 160
R = 4
FCAP = 4


conv_layout = ("NDHWC", "DHWIO", "NDHWC")


def shifted(shard, axis, by):
    count = lax.axis_size(axis)
    pairs = [(i, i + by) for i in range(count) if 0 <= i + by < count]
    return lax.ppermute(shard, axis, pairs)


def extended_2(shard, sides, width):
    for axis, dim in sides:
        count, length = (lax.axis_size(axis), shard.shape[dim])
        up = [(i, (i + 1) % count) for i in range(count - 1)]
        down = [(j, i) for i, j in up]
        last = lax.slice_in_dim(shard, length - width, length, axis=dim)
        first = lax.slice_in_dim(shard, 0, width, axis=dim)
        before = lax.ppermute(last, axis, up)
        after = lax.ppermute(first, axis, down)
        shard = jnp.concatenate([before, shard, after], axis=dim)
    return shard


def convolve(frames, kernel):
    return lax.conv_general_dilated(
        frames[None],
        kernel,
        (1, 1, 1),
        [(0, 0), (0, 0), (1, 1)],
        dimension_numbers=conv_layout,
        preferred_element_type=jnp.float32,
    )[0]


def band_tables(frame_counts):
    ends = jnp.cumsum(frame_counts)
    return (ends - frame_counts, ends)


def right_tail(frames, own_count, depth):
    zeros_front = jnp.zeros((depth,) + frames.shape[1:], frames.dtype)
    joined = jnp.concatenate([zeros_front, frames], axis=0)
    return lax.dynamic_slice_in_dim(joined, own_count, depth, 0)


def assemble(received, frame_counts, depth):
    band_index = lax.axis_index("band")
    band_count = frame_counts.shape[0]
    starts, ends = band_tables(frame_counts)
    start_here = starts[band_index]
    pieces = []
    for offset in range(depth):
        frame_at = start_here - depth + offset
        chosen = jnp.zeros_like(received[0][0])
        for distance in range(1, depth + 1):
            owner_band = band_index - distance
            clipped = jnp.clip(owner_band, 0, band_count - 1)
            inside = (owner_band >= 0) & (frame_at >= starts[clipped]) & (frame_at < ends[clipped])
            position = jnp.clip(frame_at - ends[clipped] + depth, 0, depth - 1)
            candidate = lax.dynamic_index_in_dim(
                received[distance - 1], position, 0, keepdims=False
            )
            chosen = jnp.where(inside, candidate, chosen)
        pieces.append(chosen)
    return jnp.stack(pieces)


def per_device(latents, token_cell, frame_counts, in_kernel, in_bias, mid_kernel, mid_bias):
    band_total = lax.axis_size("band")
    rows_total = lax.axis_size("rows")
    band_index = lax.axis_index("band")
    rows_index = lax.axis_index("rows")
    channels = latents.shape[1]
    span_cells = R * W // band_total
    plane_cells = R * rows_total * W
    starts, ends = band_tables(frame_counts)
    frame_of = token_cell // plane_cells
    spot_index = token_cell % span_cells
    owners = jnp.sum((frame_of[:, None] >= ends[None, :]).astype(jnp.int32), axis=1)
    onehot = (owners[:, None] == jnp.arange(band_total, dtype=jnp.int32)[None, :]).astype(jnp.int32)
    slot_of = frame_of - jnp.sum(onehot * starts[None, :], axis=1)
    position = (owners * FCAP + slot_of) * span_cells + spot_index
    outgoing = (
        jnp.zeros((band_total * FCAP * span_cells, channels), latents.dtype)
        .at[position]
        .set(latents)
    )
    outgoing = outgoing.reshape(band_total, FCAP, span_cells * channels)
    target_rows = (band_index * rows_total + rows_index) // band_total
    spread = jnp.zeros((band_total, rows_total, FCAP, 1, span_cells * channels), latents.dtype)
    spread = lax.dynamic_update_slice_in_dim(spread, outgoing[:, None, :, None, :], target_rows, 1)
    spread = spread.reshape(band_total * rows_total, FCAP, 1, span_cells * channels)
    arrived = lax.all_to_all(spread, ("band", "rows"), split_axis=0, concat_axis=2, tiled=True)
    own_block = lax.dynamic_slice_in_dim(arrived, rows_index * band_total, band_total, 2)
    grid_local = own_block.reshape(FCAP, R, W * channels)
    own_count = frame_counts[band_index]
    tail_frames = right_tail(grid_local, own_count, 2)
    received = [shifted(tail_frames, "band", distance) for distance in range(1, 3)]
    extended = jnp.concatenate([assemble(received, frame_counts, 2), grid_local], axis=0)
    extended = extended_2(extended, (("rows", 1),), 1)
    first_conv = convolve(extended.reshape(FCAP + 2, R + 2, W, channels), in_kernel) + in_bias
    active = jax.nn.silu(first_conv).astype(jnp.bfloat16)
    tail_active = right_tail(active, own_count, 2)
    received_active = [shifted(tail_active, "band", distance) for distance in range(1, 3)]
    mixing_input = jnp.concatenate([assemble(received_active, frame_counts, 2), active], axis=0)
    mixing_input = extended_2(mixing_input, (("rows", 1),), 1)
    mixed = convolve(mixing_input, mid_kernel) + mid_bias
    live_slots = jnp.arange(FCAP, dtype=jnp.int32) < own_count
    decoded = jnp.where(live_slots[:, None, None, None], mixed, 0.0).astype(jnp.bfloat16)
    return decoded


def solution(mesh):
    placed = (P(("band", "rows"), None), P(("band", "rows")), P(), P(), P(), P(), P())
    return jax.shard_map(
        per_device,
        mesh=mesh,
        in_specs=placed,
        out_specs=P("band", "rows", None, None),
        check_vma=False,
    )
```

profile of v0, /device:TPU:41, one launch (start us, length us, event | category | flops | bytes accessed | tf_op | source)
XLA Modules:
  0.0 213.8 jit_solution(9461889627069353072)
XLA Ops:
  4.1 4.5 %scatter_custom_fusion = bf16[2560,16]{1,0:T(8,128)(2,1)S(1)} fusion(s32[840]{0:T(1024)S(1)} %compare_select_fusion, bf16[840,16]{1,0:T(8,128)(2,1)S(1)} %copy.68, bf16[]{:T(256)} %constant.102.clone.1), kind=kCustom, calls=%fused_computation.33 | custom fusion | bytes 81922 | tf_op jit(solution)/shard_map/scatter | solution.py:95
  9.2 4.1 %dynamic_update_slice.3 = bf16[16,8,4,1,640]{4,1,0,2,3:T(8,128)(2,1)S(1)} dynamic-update-slice(bf16[16,8,4,1,640]{4,1,0,2,3:T(8,128)(2,1)S(1)} %broadcast_in_dim.17, bf16[16,1,4,1,640]{4,1,0,2,3:T(2,128)(2,1)S(1)} %copy.69, s32[]{:T(128)} %constant.97.clone.1, s32[]{:T(128)S(6)} %select_n.139, s32[]{:T(128)} %constant.97.clone.1, s32[]{:T(128)} %constant.97.clone.1, s32[]{:T(128)} %constant.97.clone.1) | dynamic-update-slice | bytes 163844 | tf_op jit(solution)/shard_map/dynamic_update_slice | solution.py:100
  13.4 1.3 copy.70
  14.7 10.5 %all-to-all-start = ((bf16[128,4,1,640]{3,1,2,0:T(4,128)(2,1)}), bf16[128,4,1,640]{3,1,2,0:T(4,128)(2,1)S(1)}, u32[]{:S(2)}, u32[]{:S(2)}) async-start(bf16[128,4,1,640]{3,1,2,0:T(4,128)(2,1)} %copy.70), calls=%async_computation | async-start | bytes 1310720 | tf_op jit(solution)/shard_map/all_to_all | solution.py:102
  27.9 9.2 %all-to-all-done = bf16[128,4,1,640]{3,1,2,0:T(4,128)(2,1)S(1)} async-done(((bf16[128,4,1,640]{3,1,2,0:T(4,128)(2,1)}), bf16[128,4,1,640]{3,1,2,0:T(4,128)(2,1)S(1)}, u32[]{:S(2)}, u32[]{:S(2)}) %all-to-all-start) | async-done | bytes 655392 | tf_op jit(solution)/shard_map/all_to_all | solution.py:102
  37.2 2.4 %collective-permute-start.1 = (bf16[2,4,2560]{2,1,0:T(4,128)(2,1)S(1)}, bf16[2,4,2560]{2,1,0:T(4,128)(2,1)S(1)}, u32[]{:S(2)}, u32[]{:S(2)}) collective-permute-start(bf16[2,4,2560]{2,1,0:T(4,128)(2,1)S(1)} %pad_dynamic-slice_fusion.1), channel_id=1, source_target_pairs={{0,8},{8,16},{16,24},{24,32},{32,40},{40,48},{48,56},{56,64},{64,7... | collective-permute-start | bytes 122888 | tf_op jit(solution)/shard_map/ppermute | solution.py:17
  39.6 4.5 %collective-permute-start = (bf16[2,4,2560]{2,1,0:T(4,128)(2,1)S(1)}, bf16[2,4,2560]{2,1,0:T(4,128)(2,1)S(1)}, u32[]{:S(2)}, u32[]{:S(2)}) collective-permute-start(bf16[2,4,2560]{2,1,0:T(4,128)(2,1)S(1)} %pad_dynamic-slice_fusion.1), channel_id=1, source_target_pairs={{0,16},{8,24},{16,32},{24,40},{32,48},{40,56},{48,64},{56,72},{64,... | collective-permute-start | bytes 122888 | tf_op jit(solution)/shard_map/ppermute | solution.py:17
  54.2 3.7 %collective-permute-start.2 = (bf16[6,1,2560]{2,1,0:T(2,128)(2,1)S(1)}, bf16[6,1,2560]{2,1,0:T(2,128)(2,1)S(1)}, u32[]{:S(2)}, u32[]{:S(2)}) collective-permute-start(bf16[6,1,2560]{2,1,0:T(2,128)(2,1)S(1)} %get-tuple-element.9), channel_id=1, source_target_pairs={{0,1},{1,2},{2,3},{3,4},{4,5},{5,6},{6,7},{8,9},{9,10},{10,11},{11... | collective-permute-start | bytes 92168 | tf_op jit(solution)/shard_map/ppermute | solution.py:27
  57.8 2.2 %collective-permute-start.3 = (bf16[6,1,2560]{2,1,0:T(2,128)(2,1)S(1)}, bf16[6,1,2560]{2,1,0:T(2,128)(2,1)S(1)}, u32[]{:S(2)}, u32[]{:S(2)}) collective-permute-start(bf16[6,1,2560]{2,1,0:T(2,128)(2,1)S(1)} %get-tuple-element.10), channel_id=1, source_target_pairs={{1,0},{2,1},{3,2},{4,3},{5,4},{6,5},{7,6},{9,8},{10,9},{11,10},{12... | collective-permute-start | bytes 92168 | tf_op jit(solution)/shard_map/ppermute | solution.py:28
  60.0 3.3 %collective-permute-done.3 = bf16[6,1,2560]{2,1,0:T(2,128)(2,1)S(1)} collective-permute-done((bf16[6,1,2560]{2,1,0:T(2,128)(2,1)S(1)}, bf16[6,1,2560]{2,1,0:T(2,128)(2,1)S(1)}, u32[]{:S(2)}, u32[]{:S(2)}) %collective-permute-start.3) | collective-permute-done | bytes 30752 | tf_op jit(solution)/shard_map/ppermute | solution.py:28
  64.8 1.6 pad.2
  66.4 2.4 %reshape.78 = bf16[6,6,1,8,21,16]{5,4,3,1,0,2:T(8,128)(2,1)S(1)} reshape(bf16[6,6,1,168,16]{4,3,1,0,2:T(8,128)(2,1)} %pad.2) | data formatting | bytes 387072 | tf_op jit(solution)/shard_map/conv_general_dilated | solution.py:34
  69.1 3.5 %broadcast_select_fusion = f32[4,4,8,21,384]{4,2,3,1,0:T(8,128)S(1)} fusion(pred[8,21]{0,1:T(8,128)(4,1)S(1)} %copy-done.5, bf16[3,3,3,16,384]{4,3,2,1,0:T(8,128)(2,1)S(1)} %copy-done, bf16[6,6,1,7,2,16]{5,3,4,1,0,2:T(8,128)(2,1)S(1)} %slice.22, bf16[6,6,1,8,21,16]{5,3,4,1,0,2:T(8,128)(2,1)S(1)} %copy.74), kind=kOutput, calls=%fused_computation.24 | convolution fusion | flops 893481984 | bytes 4670376 | tf_op jit(solution)/shard_map/conv_general_dilated | solution.py:34
  73.7 2.1 fusion.12
  76.4 2.8 %collective-permute-start.5 = (bf16[2,4,160,384]{3,1,2,0:T(4,128)(2,1)S(1)}, bf16[2,4,160,384]{3,1,2,0:T(4,128)(2,1)S(1)}, u32[]{:S(2)}, u32[]{:S(2)}) collective-permute-start(bf16[2,4,160,384]{3,1,2,0:T(4,128)(2,1)S(1)} %pad_dynamic-slice_fusion), channel_id=1, source_target_pairs={{0,8},{8,16},{16,24},{24,32},{32,40},{40,48},{48,56},{56,64},{64,7... | collective-permute-start | bytes 2949128 | tf_op jit(solution)/shard_map/ppermute | solution.py:17
  79.2 2.6 %collective-permute-start.4 = (bf16[2,4,160,384]{3,1,2,0:T(4,128)(2,1)S(1)}, bf16[2,4,160,384]{3,1,2,0:T(4,128)(2,1)S(1)}, u32[]{:S(2)}, u32[]{:S(2)}) collective-permute-start(bf16[2,4,160,384]{3,1,2,0:T(4,128)(2,1)S(1)} %pad_dynamic-slice_fusion), channel_id=1, source_target_pairs={{0,16},{8,24},{16,32},{24,40},{32,48},{40,56},{48,64},{56,72},{64,... | collective-permute-start | bytes 2949128 | tf_op jit(solution)/shard_map/ppermute | solution.py:17
  81.8 42.7 %collective-permute-done.5 = bf16[2,4,160,384]{3,1,2,0:T(4,128)(2,1)S(1)} collective-permute-done((bf16[2,4,160,384]{3,1,2,0:T(4,128)(2,1)S(1)}, bf16[2,4,160,384]{3,1,2,0:T(4,128)(2,1)S(1)}, u32[]{:S(2)}, u32[]{:S(2)}) %collective-permute-start.5) | collective-permute-done | bytes 983072 | tf_op jit(solution)/shard_map/ppermute | solution.py:17
  125.1 2.1 pad_maximum_fusion
  127.2 2.1 fusion.35
  129.4 2.2 %collective-permute-start.7 = (bf16[6,1,160,384]{3,2,1,0:T(8,128)(2,1)S(1)}, bf16[6,1,160,384]{3,2,1,0:T(8,128)(2,1)S(1)}, u32[]{:S(2)}, u32[]{:S(2)}) collective-permute-start(bf16[6,1,160,384]{3,2,1,0:T(8,128)(2,1)S(1)} %copy.77), channel_id=1, source_target_pairs={{1,0},{2,1},{3,2},{4,3},{5,4},{6,5},{7,6},{9,8},{10,9},{11,10},{12... | collective-permute-start | bytes 2211848 | tf_op jit(solution)/shard_map/ppermute | solution.py:28
  131.8 19.5 %collective-permute-start.6 = (bf16[6,1,160,384]{3,2,1,0:T(8,128)(2,1)S(1)}, bf16[6,1,160,384]{3,2,1,0:T(8,128)(2,1)S(1)}, u32[]{:S(2)}, u32[]{:S(2)}) collective-permute-start(bf16[6,1,160,384]{3,2,1,0:T(8,128)(2,1)S(1)} %copy.76), channel_id=1, source_target_pairs={{0,1},{1,2},{2,3},{3,4},{4,5},{5,6},{6,7},{8,9},{9,10},{10,11},{11... | collective-permute-start | bytes 2211848 | tf_op jit(solution)/shard_map/ppermute | solution.py:27
  154.3 5.5 %maximum_bitcast_fusion = bf16[6,6,1,160,384]{4,1,3,0,2:T(8,128)(2,1)S(1)} fusion(bf16[6,1,160,384]{3,1,2,0:T(2,128)(2,1)S(1)} %copy.79, bf16[4,4,160,384]{3,1,2,0:T(4,128)(2,1)S(1)} %fusion.12, bf16[1,4,160,384]{3,1,2,0:T(4,128)(2,1)S(1)} %get-tuple-element.8, bf16[1,4,160,384]{3,1,2,0:T(4,128)(2,1)S(1)} %get-tuple-element.7, ...), kind=kLoop, calls=%fused_computation.3 | loop fusion | flops 22118400 | bytes 8847360 | tf_op jit(solution)/shard_map/broadcast_in_dim | solution.py:35
  161.5 48.5 %fusion.15 = f32[4,4,8,21,384]{4,2,3,1,0:T(8,128)S(1)} fusion(bf16[3,3,3,384,384]{4,3,2,1,0:T(8,128)(2,1)} %param.12, bf16[6,6,1,7,2,384]{5,3,4,1,0,2:T(8,128)(2,1)S(1)} %slice.26, bf16[6,6,1,8,21,384]{5,3,4,1,0,2:T(8,128)(2,1)S(1)} %copy.82, pred[8,21]{0,1:T(8,128)(4,1)S(1)} %copy-done.5), kind=kOutput, calls=%fused_computation.23 | convolution fusion | flops 21419827200 | bytes 17123496 | tf_op jit(solution)/shard_map/conv_general_dilated | solution.py:34
  212.0 1.5 copy.84
  (57 shorter events, 17.7 us)
Async XLA Ops:
  0.0 69.1 %copy-start = (bf16[3,3,3,16,384]{4,3,2,1,0:T(8,128)(2,1)S(1)}, bf16[3,3,3,16,384]{4,3,2,1,0:T(8,128)(2,1)}, u32[]{:S(2)}) copy-start(bf16[3,3,3,16,384]{4,3,2,1,0:T(8,128)(2,1)} %param.10) | copy-start | bytes 995332
  0.0 25.2 %copy-start.4 = (s32[16]{0:T(128)S(1)}, s32[16]{0:T(128)}, u32[]{:S(2)}) copy-start(s32[16]{0:T(128)} %param.9) | copy-start | bytes 196
  14.7 22.4 %all-to-all-start = ((bf16[128,4,1,640]{3,1,2,0:T(4,128)(2,1)}), bf16[128,4,1,640]{3,1,2,0:T(4,128)(2,1)S(1)}, u32[]{:S(2)}, u32[]{:S(2)}) async-start(bf16[128,4,1,640]{3,1,2,0:T(4,128)(2,1)} %copy.70), calls=%async_computation | async-start | bytes 1310720 | tf_op jit(solution)/shard_map/all_to_all | solution.py:102
  37.2 16.7 %collective-permute-start.1 = (bf16[2,4,2560]{2,1,0:T(4,128)(2,1)S(1)}, bf16[2,4,2560]{2,1,0:T(4,128)(2,1)S(1)}, u32[]{:S(2)}, u32[]{:S(2)}) collective-permute-start(bf16[2,4,2560]{2,1,0:T(4,128)(2,1)S(1)} %pad_dynamic-slice_fusion.1), channel_id=1, source_target_pairs={{0,8},{8,16},{16,24},{24,32},{32,40},{40,48},{48,56},{56,64},{64,7... | collective-permute-start | bytes 122888 | tf_op jit(solution)/shard_map/ppermute | solution.py:17
  39.6 14.3 %collective-permute-start = (bf16[2,4,2560]{2,1,0:T(4,128)(2,1)S(1)}, bf16[2,4,2560]{2,1,0:T(4,128)(2,1)S(1)}, u32[]{:S(2)}, u32[]{:S(2)}) collective-permute-start(bf16[2,4,2560]{2,1,0:T(4,128)(2,1)S(1)} %pad_dynamic-slice_fusion.1), channel_id=1, source_target_pairs={{0,16},{8,24},{16,32},{24,40},{32,48},{40,56},{48,64},{56,72},{64,... | collective-permute-start | bytes 122888 | tf_op jit(solution)/shard_map/ppermute | solution.py:17
  54.2 5.9 %collective-permute-start.2 = (bf16[6,1,2560]{2,1,0:T(2,128)(2,1)S(1)}, bf16[6,1,2560]{2,1,0:T(2,128)(2,1)S(1)}, u32[]{:S(2)}, u32[]{:S(2)}) collective-permute-start(bf16[6,1,2560]{2,1,0:T(2,128)(2,1)S(1)} %get-tuple-element.9), channel_id=1, source_target_pairs={{0,1},{1,2},{2,3},{3,4},{4,5},{5,6},{6,7},{8,9},{9,10},{10,11},{11... | collective-permute-start | bytes 92168 | tf_op jit(solution)/shard_map/ppermute | solution.py:27
  57.8 5.5 %collective-permute-start.3 = (bf16[6,1,2560]{2,1,0:T(2,128)(2,1)S(1)}, bf16[6,1,2560]{2,1,0:T(2,128)(2,1)S(1)}, u32[]{:S(2)}, u32[]{:S(2)}) collective-permute-start(bf16[6,1,2560]{2,1,0:T(2,128)(2,1)S(1)} %get-tuple-element.10), channel_id=1, source_target_pairs={{1,0},{2,1},{3,2},{4,3},{5,4},{6,5},{7,6},{9,8},{10,9},{11,10},{12... | collective-permute-start | bytes 92168 | tf_op jit(solution)/shard_map/ppermute | solution.py:28
  66.4 2.7 %copy-start.5 = (pred[8,21]{0,1:T(8,128)(4,1)S(1)}, pred[8,21]{0,1:T(8,128)(4,1)}, u32[]{:S(2)}) copy-start(pred[8,21]{0,1:T(8,128)(4,1)} %constant.131) | copy-start | bytes 508
  72.6 1.1 copy-start.2
  76.4 48.2 %collective-permute-start.5 = (bf16[2,4,160,384]{3,1,2,0:T(4,128)(2,1)S(1)}, bf16[2,4,160,384]{3,1,2,0:T(4,128)(2,1)S(1)}, u32[]{:S(2)}, u32[]{:S(2)}) collective-permute-start(bf16[2,4,160,384]{3,1,2,0:T(4,128)(2,1)S(1)} %pad_dynamic-slice_fusion), channel_id=1, source_target_pairs={{0,8},{8,16},{16,24},{24,32},{32,40},{40,48},{48,56},{56,64},{64,7... | collective-permute-start | bytes 2949128 | tf_op jit(solution)/shard_map/ppermute | solution.py:17
  79.2 45.4 %collective-permute-start.4 = (bf16[2,4,160,384]{3,1,2,0:T(4,128)(2,1)S(1)}, bf16[2,4,160,384]{3,1,2,0:T(4,128)(2,1)S(1)}, u32[]{:S(2)}, u32[]{:S(2)}) collective-permute-start(bf16[2,4,160,384]{3,1,2,0:T(4,128)(2,1)S(1)} %pad_dynamic-slice_fusion), channel_id=1, source_target_pairs={{0,16},{8,24},{16,32},{24,40},{32,48},{40,56},{48,64},{56,72},{64,... | collective-permute-start | bytes 2949128 | tf_op jit(solution)/shard_map/ppermute | solution.py:17
  129.4 22.5 %collective-permute-start.7 = (bf16[6,1,160,384]{3,2,1,0:T(8,128)(2,1)S(1)}, bf16[6,1,160,384]{3,2,1,0:T(8,128)(2,1)S(1)}, u32[]{:S(2)}, u32[]{:S(2)}) collective-permute-start(bf16[6,1,160,384]{3,2,1,0:T(8,128)(2,1)S(1)} %copy.77), channel_id=1, source_target_pairs={{1,0},{2,1},{3,2},{4,3},{5,4},{6,5},{7,6},{9,8},{10,9},{11,10},{12... | collective-permute-start | bytes 2211848 | tf_op jit(solution)/shard_map/ppermute | solution.py:28
  131.8 21.3 %collective-permute-start.6 = (bf16[6,1,160,384]{3,2,1,0:T(8,128)(2,1)S(1)}, bf16[6,1,160,384]{3,2,1,0:T(8,128)(2,1)S(1)}, u32[]{:S(2)}, u32[]{:S(2)}) collective-permute-start(bf16[6,1,160,384]{3,2,1,0:T(8,128)(2,1)S(1)} %copy.76), channel_id=1, source_target_pairs={{0,1},{1,2},{2,3},{3,4},{4,5},{5,6},{6,7},{8,9},{9,10},{10,11},{11... | collective-permute-start | bytes 2211848 | tf_op jit(solution)/shard_map/ppermute | solution.py:27
  210.0 1.1 copy-start.3
  211.1 2.5 %copy-start.1 = (bf16[3,3,3,16,384]{4,3,2,1,0:T(8,128)(2,1)S(1)}, bf16[3,3,3,16,384]{4,3,2,1,0:T(8,128)(2,1)}, u32[]{:S(2)}) copy-start(bf16[3,3,3,16,384]{4,3,2,1,0:T(8,128)(2,1)} %param.10) | copy-start | bytes 995332
where the time goes:
time: 214 us
  waiting for transfers between devices  55.3 us (26%)
  matrix products  52 us (24%)
  starting transfers between devices  50.3 us (24%)
  local copies, waits for them, and re-layouts  30.4 us (14%)
  other arithmetic  14.6 us (7%)
  between operations  11.3 us (5%)
    conv_general_dilated x2, matrix products, convolve(): lax.conv_general_dilated(frames[None], kernel, (1, 1, 1), [(0, 0), (0, 0)...  52 us
    ppermute x4, waiting for transfers between devices, shifted(): return lax.ppermute(shard, axis, pairs)  42.7 us
    ppermute x2, starting transfers between devices, extended_2(): before = lax.ppermute(last, axis, up)  23.1 us
    ppermute x4, starting transfers between devices, shifted(): return lax.ppermute(shard, axis, pairs)  12.3 us
    all_to_all x1, starting transfers between devices, per_device(): lax.all_to_all(spread, ('band', 'rows'), split_axis=0, concat_axis=2, til...  10.5 us
    all_to_all x1, waiting for transfers between devices, per_device(): lax.all_to_all(spread, ('band', 'rows'), split_axis=0, concat_axis=2, til...  9.19 us
    conv_general_dilated x7, local copies, waits for them, and re-layouts, convolve(): lax.conv_general_dilated(frames[None], kernel, (1, 1, 1), [(0, 0), (0, 0)...  5.5 us
    broadcast_in_dim x1, other arithmetic, convolve(): frames[None]  5.45 us
  transfers between devices with their start and end apart: 9, of which 3 were waited for; matrix products, arithmetic and copies ran while one was open for 2% of the time, Pallas kernels for 0%

commit v1 on v0

v1 whole, which is shorter than its diff:
```python
import functools

import jax
import jax.numpy as jnp
from jax import lax
from jax.experimental import pallas as pl
from jax.experimental.pallas import tpu as pltpu
from jax.sharding import PartitionSpec as P

W = 160
R = 4
FCAP = 4
Z = 16
C = 384
SPAN = 40
BANDS = 16
ROWS = 8
TOK = 840
LANES = 128
ACT_FRAMES = FCAP + 2
ACT_ROWS = R + 2
LAT_ROWS = R + 4
SLAB = R * W
K2 = 9 * C


def sort_kernel(counts, cell_ref, lat_ref, out_ref, flat):
    device = lax.axis_index("band") * ROWS + lax.axis_index("rows")
    cell = cell_ref[...]
    frame = ((cell >> 10) * 205) >> 10
    spot = cell - frame * (W * R * ROWS) - device * SPAN
    lat = lat_ref[...]
    zero = jnp.zeros_like(lat)
    frame_b = jnp.broadcast_to(frame, (Z, TOK))
    spread = jnp.concatenate(
        [jnp.where(frame_b == (f - FCAP), lat, zero) for f in range(32)], axis=0
    )
    spots = lax.broadcasted_iota(jnp.int32, (SPAN, TOK), 0)
    pick = jnp.where(spots == jnp.broadcast_to(spot, (SPAN, TOK)), 1.0, 0.0).astype(jnp.bfloat16)
    sorted_rows = lax.dot_general(
        pick, spread, (((1,), (1,)), ((), ())), preferred_element_type=jnp.float32
    )
    for tile in range(4):
        flat[tile] = sorted_rows[:, tile * LANES:(tile + 1) * LANES]
    lane = lax.broadcasted_iota(jnp.int32, (SPAN, LANES), 1)
    start = jnp.int32(0)
    for band in range(BANDS):
        tile = start // 8
        turn = (start - tile * 8) * Z
        back = jnp.where(turn == 0, 0, LANES - turn)
        left = pltpu.roll(flat[tile], back, 1)
        right = pltpu.roll(flat[jnp.minimum(tile + 1, 3)], back, 1)
        window = jnp.where(lane < LANES - turn, left, right)
        out_ref[band] = window.astype(jnp.bfloat16)
        start = start + counts[band]


def sort_tokens(counts, cells, latents):
    return pl.pallas_call(
        sort_kernel,
        in_specs=[
            pl.BlockSpec(memory_space=pltpu.SMEM),
            pl.BlockSpec(memory_space=pltpu.VMEM),
            pl.BlockSpec(memory_space=pltpu.VMEM),
        ],
        out_specs=pl.BlockSpec(memory_space=pltpu.VMEM),
        out_shape=jax.ShapeDtypeStruct((BANDS, SPAN, LANES), jnp.bfloat16),
        scratch_shapes=[pltpu.VMEM((4, SPAN, LANES), jnp.float32)],
        name="sort_tokens",
    )(counts, cells, latents)


def conv_kernel(
    counts, got_ref, w1_ref, b1_ref, b2_ref, w2_hbm, out_hbm,
    w2, flat, e01, e2, act, patches, outs, w2_sem, out_sem,
):
    band = lax.axis_index("band")
    rows = lax.axis_index("rows")
    fetch = pltpu.make_async_copy(w2_hbm, w2, w2_sem)
    fetch.start()
    start = jnp.int32(0)
    own = jnp.int32(0)
    for b in range(BANDS):
        start = start + jnp.where(b < band, counts[b], 0)
        own = own + jnp.where(b == band, counts[b], 0)

    lane = lax.broadcasted_iota(jnp.int32, (W, LANES), 1)
    low = lane < 64
    flat[:, 0:8, :] = jnp.zeros((2, 8, LANES), jnp.float32)
    flat[:, 168:176, :] = jnp.zeros((2, 8, LANES), jnp.float32)
    after = jnp.zeros((W, LANES), jnp.float32)
    for i in reversed(range(LAT_ROWS)):
        buf = i % 2
        for q in range(4):
            piece = got_ref[4 * (i % 2) + q, i // 2]
            flat[buf, 8 + SPAN * q:8 + SPAN * (q + 1), :] = piece.astype(jnp.float32)
        left = flat[buf, 7:167, :]
        mid = flat[buf, 8:168, :]
        right = flat[buf, 9:169, :]
        for pp in range(3):
            down = (LANES - 32 * pp) % LANES
            up = (64 + LANES - 32 * pp) % LANES
            first = jnp.where(low, pltpu.roll(left, down, 1), pltpu.roll(mid, up, 1))
            second = jnp.where(low, pltpu.roll(right, down, 1), pltpu.roll(after, up, 1))
            e01[pp, W * i:W * (i + 1), :] = first.astype(jnp.bfloat16)
            e2[pp, W * i:W * (i + 1), :] = second.astype(jnp.bfloat16)
        after = right

    act[:, 0:8, :] = jnp.zeros((3, 8, 2 * C), jnp.float32)
    act[:, 168:176, :] = jnp.zeros((3, 8, 2 * C), jnp.float32)

    def first_rows(i, carry):
        row = R * rows - 1 + i
        row_in = (row >= 0) & (row < R * ROWS)
        for pp in range(3):
            at = [pl.ds(pl.multiple_of(W * (i + k), W), W) for k in range(3)]
            lhs = jnp.concatenate(
                [e01[pp, at[0], :], e01[pp, at[1], :], e01[pp, at[2], :],
                 e2[pp, at[0], :], e2[pp, at[2], :]], axis=1)
            total = jnp.dot(lhs, w1_ref[...], preferred_element_type=jnp.float32)
            for half in range(2):
                p = 2 * pp + half
                cols = slice(half * C, (half + 1) * C)
                v = total[:, cols] + b1_ref[...]
                v = v / (1.0 + jnp.exp(-v))
                keep = row_in & (start - 2 + p >= 0)
                act[pp, 8:168, cols] = jnp.where(keep, v, 0.0)
                for e in range(3):
                    patches[p, at[0], e * C:(e + 1) * C] = (
                        act[pp, 7 + e:167 + e, cols].astype(jnp.bfloat16))
        return carry

    lax.fori_loop(0, ACT_ROWS, first_rows, 0)
    fetch.wait()

    def lhs_of(p):
        return jnp.concatenate(
            [patches[p, W * b:W * b + SLAB, :] for b in range(3)], axis=1)

    def pair(n0, carry):
        @pl.when(own > n0)
        def _():
            a0 = jnp.dot(lhs_of(n0), w2[0], preferred_element_type=jnp.float32)
            t = jnp.dot(
                lhs_of(n0 + 1), jnp.concatenate([w2[1], w2[0]], axis=1),
                preferred_element_type=jnp.float32)
            a0 += t[:, :C]
            a1 = t[:, C:]
            t = jnp.dot(
                lhs_of(n0 + 2), jnp.concatenate([w2[2], w2[1]], axis=1),
                preferred_element_type=jnp.float32)
            a0 += t[:, :C]
            a1 += t[:, C:]
            a1 += jnp.dot(lhs_of(n0 + 3), w2[2], preferred_element_type=jnp.float32)
            outs[n0] = (a0 + b2_ref[...]).astype(jnp.bfloat16)
            outs[n0 + 1] = jnp.where(own > n0 + 1, a1 + b2_ref[...], 0.0).astype(jnp.bfloat16)

        @pl.when(own <= n0)
        def _():
            outs[pl.ds(n0, 2)] = jnp.zeros((2, SLAB, C), jnp.bfloat16)

        pltpu.make_async_copy(
            outs.at[pl.ds(n0, 2)], out_hbm.at[pl.ds(n0, 2)], out_sem.at[n0 // 2]).start()
        return carry

    lax.fori_loop(0, 2, lambda k, c: pair(2 * k, c), 0)
    for k in range(2):
        pltpu.make_async_copy(
            outs.at[pl.ds(2 * k, 2)], out_hbm.at[pl.ds(2 * k, 2)], out_sem.at[k]).wait()


def convs(counts, got, w1, b1, b2, w2):
    vmem = pl.BlockSpec(memory_space=pltpu.VMEM)
    return pl.pallas_call(
        conv_kernel,
        in_specs=[
            pl.BlockSpec(memory_space=pltpu.SMEM), vmem, vmem, vmem, vmem,
            pl.BlockSpec(memory_space=pl.ANY),
        ],
        out_specs=pl.BlockSpec(memory_space=pl.ANY),
        out_shape=jax.ShapeDtypeStruct((FCAP, SLAB, C), jnp.bfloat16),
        scratch_shapes=[
            pltpu.VMEM((3, K2, C), jnp.bfloat16),
            pltpu.VMEM((2, 176, LANES), jnp.float32),
            pltpu.VMEM((3, LAT_ROWS * W, LANES), jnp.bfloat16),
            pltpu.VMEM((3, LAT_ROWS * W, LANES), jnp.bfloat16),
            pltpu.VMEM((3, 176, 2 * C), jnp.float32),
            pltpu.VMEM((ACT_FRAMES, ACT_ROWS * W, 3 * C), jnp.bfloat16),
            pltpu.VMEM((FCAP, SLAB, C), jnp.bfloat16),
            pltpu.SemaphoreType.DMA,
            pltpu.SemaphoreType.DMA((2,)),
        ],
        compiler_params=pltpu.CompilerParams(vmem_limit_bytes=56 * 1024 * 1024),
        name="two_convs",
    )(counts, got, w1, b1, b2, w2)


def frame_pair_kernel(in_kernel):
    taps = jnp.transpose(in_kernel, (1, 2, 0, 3, 4)).reshape(3, 3, 3 * Z, C)
    even = jnp.pad(taps, ((0, 0), (0, 0), (0, Z), (0, 0)))
    odd = jnp.pad(taps, ((0, 0), (0, 0), (Z, 0), (0, 0)))
    both = jnp.concatenate([even, odd], axis=-1)
    return jnp.concatenate(
        [both[:, :2].reshape(384, 2 * C), both[:, 2].reshape(192, 2 * C),
         jnp.zeros((64, 2 * C), in_kernel.dtype)], axis=0)


def per_device(latents, token_cell, frame_counts, in_kernel, in_bias, mid_kernel, mid_bias):
    windows = sort_tokens(frame_counts, token_cell.reshape(1, TOK), latents.T)
    by_band = lax.all_to_all(windows, "band", split_axis=0, concat_axis=0, tiled=True)
    edged = jnp.pad(by_band, ((1, 1), (0, 0), (0, 0)))
    spread = jnp.stack([edged[k:k + 15:2] for k in range(4)], axis=1)
    got = lax.all_to_all(spread, "rows", split_axis=0, concat_axis=0, tiled=True)
    out = convs(
        frame_counts, got, frame_pair_kernel(in_kernel), in_bias.reshape(1, C),
        mid_bias.reshape(1, C), mid_kernel.reshape(3, K2, C))
    return out.reshape(FCAP, R, W, C)


def solution(mesh):
    placed = (P(("band", "rows"), None), P(("band", "rows")), P(), P(), P(), P(), P())
    return jax.shard_map(
        per_device,
        mesh=mesh,
        in_specs=placed,
        out_specs=P("band", "rows", None, None),
        check_vma=False,
    )
```

time: 214 us -> 66.5 us (0.31)
  the two profiles are of different devices: /device:TPU:41 before, /device:TPU:4 now
where the time goes in v1:
time: 66.5 us; the launch traced here: 66 us
  Pallas kernels  36.2 us (54%)
  starting transfers between devices  12.9 us (19%)
  waiting for transfers between devices  10.5 us (16%)
  local copies, waits for them, and re-layouts  4.35 us (7%)
  other arithmetic  2.03 us (3%)
    pallas_call x1, Pallas kernels, convs(): pl.pallas_call(conv_kernel, in_specs=[pl.BlockSpec(memory_space=pltpu.SME...  34.3 us
    all_to_all x1, starting transfers between devices, per_device(): lax.all_to_all(windows, 'band', split_axis=0, concat_axis=0, tiled=True)  8.29 us
    all_to_all x1, waiting for transfers between devices, per_device(): lax.all_to_all(spread, 'rows', split_axis=0, concat_axis=0, tiled=True)  5.62 us
    all_to_all x1, waiting for transfers between devices, per_device(): lax.all_to_all(windows, 'band', split_axis=0, concat_axis=0, tiled=True)  4.86 us
    all_to_all x1, starting transfers between devices, per_device(): lax.all_to_all(spread, 'rows', split_axis=0, concat_axis=0, tiled=True)  4.6 us
    pallas_call x1, Pallas kernels, sort_tokens(): pl.pallas_call(sort_kernel, in_specs=[pl.BlockSpec(memory_space=pltpu.SME...  1.99 us
    unnamed x7, local copies, waits for them, and re-layouts  1.73 us
  transfers between devices with their start and end apart: 2, of which 2 were waited for; matrix products, arithmetic and copies ran while one was open for 5% of the time, Pallas kernels for 0%

profile of v1, /device:TPU:4, one launch (start us, length us, event | category | flops | bytes accessed | tf_op | source)
XLA Modules:
  0.0 66.0 jit_solution(8151694346367648361)
XLA Ops:
  0.0 1.3 %reshape.21.cell_ref = s32[1,840]{1,0:T(1,128)} reshape(s32[840]{0:T(1024)} %param.8) | data formatting | bytes 6720 | tf_op jit(solution)/shard_map/reshape | solution.py:209
  1.3 2.0 %sort_tokens.1 = bf16[16,40,128]{2,1,0:T(8,128)(2,1)} custom-call(s32[16]{0:T(128)} %counts.3, s32[1,840]{1,0:T(1,128)} %reshape.21.cell_ref, bf16[16,840]{1,0:T(8,128)(2,1)} %bitcast.26), custom_call_target="tpu_custom_call" | custom-call | tf_op jit(solution)/shard_map/sort_tokens/pallas_call | solution.py:59
  3.3 8.3 %all-to-all-start = ((bf16[16,40,128]{2,1,0:T(8,128)(2,1)}), bf16[16,40,128]{2,1,0:T(8,128)(2,1)S(1)}, u32[]{:S(2)}, u32[]{:S(2)}) async-start(bf16[16,40,128]{2,1,0:T(8,128)(2,1)} %sort_tokens.1), calls=%async_computation | async-start | bytes 327680 | tf_op jit(solution)/shard_map/all_to_all | solution.py:210
  11.6 1.0 %copy.15 = bf16[3,3,3,16,384]{4,3,0,2,1:T(8,128)(2,1)S(1)} copy(bf16[3,3,3,16,384]{4,3,2,1,0:T(8,128)(2,1)} %param.10) | data formatting | bytes 663552 | tf_op args[3]
  12.6 4.9 %all-to-all-done = bf16[16,40,128]{2,1,0:T(8,128)(2,1)S(1)} async-done(((bf16[16,40,128]{2,1,0:T(8,128)(2,1)}), bf16[16,40,128]{2,1,0:T(8,128)(2,1)S(1)}, u32[]{:S(2)}, u32[]{:S(2)}) %all-to-all-start) | async-done | bytes 163872 | tf_op jit(solution)/shard_map/all_to_all | solution.py:210
  17.5 0.8 %pad_maximum_fusion = bf16[8,4,40,128]{3,2,1,0:T(8,128)(2,1)} fusion(bf16[8,1,40,128]{3,2,1,0:T(8,128)(2,1)S(1)} %get-tuple-element.8, bf16[8,1,40,128]{3,2,1,0:T(8,128)(2,1)S(1)} %get-tuple-element.7, bf16[8,1,40,128]{3,2,1,0:T(8,128)(2,1)S(1)} %get-tuple-element.6, bf16[8,1,40,128]{3,2,1,0:T(8,128)(2,1)S(1)} %get-tuple-element.5), kind=kLoop, calls=%fused_computation.6 | loop fusion | flops 491520 | bytes 655360 | tf_op jit(solution)/shard_map/stack | solution.py:212
  18.2 0.0 copy-start.1
  18.2 0.0 copy-start.2
  18.2 4.6 %all-to-all-start.1 = ((bf16[8,4,40,128]{3,2,1,0:T(8,128)(2,1)}), bf16[8,4,40,128]{3,2,1,0:T(8,128)(2,1)S(1)}, u32[]{:S(2)}, u32[]{:S(2)}) async-start(bf16[8,4,40,128]{3,2,1,0:T(8,128)(2,1)} %pad_maximum_fusion), calls=%async_computation.1 | async-start | bytes 655360 | tf_op jit(solution)/shard_map/all_to_all | solution.py:213
  22.8 0.1 fusion.2
  23.0 0.0 copy-done.1
  23.0 0.6 reshape.24.b1_ref
  23.6 0.0 copy-done.2
  23.6 0.6 reshape.25.b2_ref
  24.2 0.1 pad.17.clone
  24.3 1.2 %maximum_maximum_fusion.w1_ref = bf16[640,768]{1,0:T(8,128)(2,1)} fusion(bf16[192,768]{1,0:T(8,128)(2,1)S(1)} %bitcast.25, bf16[384,768]{1,0:T(8,128)(2,1)S(1)} %bitcast.23, bf16[640]{0:T(1024)(128)(2,1)S(1)} %pad.17.clone), kind=kLoop, calls=%fused_computation.4 | loop fusion | flops 2949120 | bytes 1869056 | tf_op jit(solution)/shard_map/concatenate | solution.py:203
  25.4 5.6 %all-to-all-done.1.got_ref = bf16[8,4,40,128]{3,2,1,0:T(8,128)(2,1)S(1)} async-done(((bf16[8,4,40,128]{3,2,1,0:T(8,128)(2,1)}), bf16[8,4,40,128]{3,2,1,0:T(8,128)(2,1)S(1)}, u32[]{:S(2)}, u32[]{:S(2)}) %all-to-all-start.1) | async-done | bytes 327712 | tf_op jit(solution)/shard_map/all_to_all | solution.py:213
  31.1 0.0 copy-start
  31.1 0.7 %copy-done = bf16[8,4,40,128]{3,2,1,0:T(8,128)(2,1)} copy-done((bf16[8,4,40,128]{3,2,1,0:T(8,128)(2,1)}, bf16[8,4,40,128]{3,2,1,0:T(8,128)(2,1)S(1)}, u32[]{:S(2)}) %copy-start) | copy-done | bytes 327704
  31.8 34.3 %two_convs.1 = bf16[4,640,384]{2,1,0:T(8,128)(2,1)} custom-call(s32[16]{0:T(128)} %counts.3, bf16[8,4,40,128]{3,2,1,0:T(8,128)(2,1)} %copy-done, bf16[640,768]{1,0:T(8,128)(2,1)} %maximum_maximum_fusion.w1_ref, f32[1,384]{1,0:T(1,128)} %reshape.24.b1_ref, f32[1,384]{1,0:T(1,128)} %reshape.25.b2_ref, bf16[3,3456,384]{2,1,0:T(8,128)(2,1)} %bitcast.22), custom_call_target="tpu_custom_call" | custom-call | tf_op jit(solution)/shard_map/two_convs/pallas_call | solution.py:174
  (4 shorter events, 0.1 us)
Async XLA Ops:
  3.3 14.2 %all-to-all-start = ((bf16[16,40,128]{2,1,0:T(8,128)(2,1)}), bf16[16,40,128]{2,1,0:T(8,128)(2,1)S(1)}, u32[]{:S(2)}, u32[]{:S(2)}) async-start(bf16[16,40,128]{2,1,0:T(8,128)(2,1)} %sort_tokens.1), calls=%async_computation | async-start | bytes 327680 | tf_op jit(solution)/shard_map/all_to_all | solution.py:210
  18.2 4.8 %copy-start.1 = (f32[384]{0:T(512)S(1)}, f32[384]{0:T(512)}, u32[]{:S(2)}) copy-start(f32[384]{0:T(512)} %param.11) | copy-start | bytes 4612
  18.2 5.4 %copy-start.2 = (f32[384]{0:T(512)S(1)}, f32[384]{0:T(512)}, u32[]{:S(2)}) copy-start(f32[384]{0:T(512)} %param.13) | copy-start | bytes 4612
  18.2 12.8 %all-to-all-start.1 = ((bf16[8,4,40,128]{3,2,1,0:T(8,128)(2,1)}), bf16[8,4,40,128]{3,2,1,0:T(8,128)(2,1)S(1)}, u32[]{:S(2)}, u32[]{:S(2)}) async-start(bf16[8,4,40,128]{3,2,1,0:T(8,128)(2,1)} %pad_maximum_fusion), calls=%async_computation.1 | async-start | bytes 655360 | tf_op jit(solution)/shard_map/all_to_all | solution.py:213
  31.1 0.7 %copy-start = (bf16[8,4,40,128]{3,2,1,0:T(8,128)(2,1)}, bf16[8,4,40,128]{3,2,1,0:T(8,128)(2,1)S(1)}, u32[]{:S(2)}) copy-start(bf16[8,4,40,128]{3,2,1,0:T(8,128)(2,1)S(1)} %all-to-all-done.1.got_ref) | copy-start | bytes 983044

commit v2 on v1

--- a/solution.py
+++ b/solution.py
@@ -17,6 +17,9 @@
 ROWS = 8
 TOK = 840
 LANES = 128
+PHASES = 5
+STEPS = W // PHASES
+WIDE = W + 2 * STEPS
 ACT_FRAMES = FCAP + 2
 ACT_ROWS = R + 2
 LAT_ROWS = R + 4
@@ -26,17 +29,17 @@
 
 def sort_kernel(counts, cell_ref, lat_ref, out_ref, flat):
     device = lax.axis_index("band") * ROWS + lax.axis_index("rows")
-    cell = cell_ref[...]
+    cell = jnp.broadcast_to(cell_ref[...].reshape(1, TOK), (Z, TOK))
     frame = ((cell >> 10) * 205) >> 10
-    spot = cell - frame * (W * R * ROWS) - device * SPAN
+    spot = (cell - frame * (W * R * ROWS) - device * SPAN)[0:1]
     lat = lat_ref[...]
     zero = jnp.zeros_like(lat)
-    frame_b = jnp.broadcast_to(frame, (Z, TOK))
     spread = jnp.concatenate(
-        [jnp.where(frame_b == (f - FCAP), lat, zero) for f in range(32)], axis=0
+        [jnp.where(frame == (f - FCAP), lat, zero) for f in range(32)], axis=0
     )
-    spots = lax.broadcasted_iota(jnp.int32, (SPAN, TOK), 0)
-    pick = jnp.where(spots == jnp.broadcast_to(spot, (SPAN, TOK)), 1.0, 0.0).astype(jnp.bfloat16)
+    place = lax.broadcasted_iota(jnp.int32, (SPAN, TOK), 0)
+    wanted = (place & 7) * PHASES + (place >> 3)
+    pick = jnp.where(wanted == jnp.broadcast_to(spot, (SPAN, TOK)), 1.0, 0.0).astype(jnp.bfloat16)
     sorted_rows = lax.dot_general(
         pick, spread, (((1,), (1,)), ((), ())), preferred_element_type=jnp.float32
     )
@@ -70,9 +73,17 @@
     )(counts, cells, latents)
 
 
+def with_edges(rows):
+    width = rows.shape[1]
+    u = lax.broadcasted_iota(jnp.int32, (STEPS, width), 0)
+    before = jnp.where(u == 0, 0.0, pltpu.roll(rows[W - STEPS:], 1, 0))
+    after = jnp.where(u == STEPS - 1, 0.0, pltpu.roll(rows[:STEPS], STEPS - 1, 0))
+    return jnp.concatenate([before, rows, after], axis=0)
+
+
 def conv_kernel(
     counts, got_ref, w1_ref, b1_ref, b2_ref, w2_hbm, out_hbm,
-    w2, flat, e01, e2, act, patches, outs, w2_sem, out_sem,
+    w2, e01, e2, patches, natural, outs, w2_sem, out_sem,
 ):
     band = lax.axis_index("band")
     rows = lax.axis_index("rows")
@@ -86,56 +97,62 @@
 
     lane = lax.broadcasted_iota(jnp.int32, (W, LANES), 1)
     low = lane < 64
-    flat[:, 0:8, :] = jnp.zeros((2, 8, LANES), jnp.float32)
-    flat[:, 168:176, :] = jnp.zeros((2, 8, LANES), jnp.float32)
-    after = jnp.zeros((W, LANES), jnp.float32)
+    above = [jnp.zeros((W, LANES), jnp.float32)] * 4
     for i in reversed(range(LAT_ROWS)):
-        buf = i % 2
-        for q in range(4):
-            piece = got_ref[4 * (i % 2) + q, i // 2]
-            flat[buf, 8 + SPAN * q:8 + SPAN * (q + 1), :] = piece.astype(jnp.float32)
-        left = flat[buf, 7:167, :]
-        mid = flat[buf, 8:168, :]
-        right = flat[buf, 9:169, :]
+        pieces = [got_ref[4 * (i % 2) + q, i // 2].astype(jnp.float32) for q in range(4)]
+        line = with_edges(jnp.concatenate(
+            [pieces[q][8 * v:8 * v + 8] for v in range(PHASES) for q in range(4)], axis=0))
+        turned = [line] + [pltpu.roll(line, 32 * k, 1) for k in range(1, 4)]
         for pp in range(3):
-            down = (LANES - 32 * pp) % LANES
-            up = (64 + LANES - 32 * pp) % LANES
-            first = jnp.where(low, pltpu.roll(left, down, 1), pltpu.roll(mid, up, 1))
-            second = jnp.where(low, pltpu.roll(right, down, 1), pltpu.roll(after, up, 1))
-            e01[pp, W * i:W * (i + 1), :] = first.astype(jnp.bfloat16)
-            e2[pp, W * i:W * (i + 1), :] = second.astype(jnp.bfloat16)
-        after = right
-
-    act[:, 0:8, :] = jnp.zeros((3, 8, 2 * C), jnp.float32)
-    act[:, 168:176, :] = jnp.zeros((3, 8, 2 * C), jnp.float32)
-
-    def first_rows(i, carry):
-        row = R * rows - 1 + i
-        row_in = (row >= 0) & (row < R * ROWS)
-        for pp in range(3):
-            at = [pl.ds(pl.multiple_of(W * (i + k), W), W) for k in range(3)]
-            lhs = jnp.concatenate(
-                [e01[pp, at[0], :], e01[pp, at[1], :], e01[pp, at[2], :],
-                 e2[pp, at[0], :], e2[pp, at[2], :]], axis=1)
-            total = jnp.dot(lhs, w1_ref[...], preferred_element_type=jnp.float32)
+            down = (4 - pp) % 4
+            up = (2 + 4 - pp) % 4
+            first = jnp.where(low, turned[down][0:W], turned[up][STEPS:STEPS + W])
+            second = jnp.where(low, turned[down][2 * STEPS:], above[up])
+            e01[pp, i] = first.astype(jnp.bfloat16)
+            e2[pp, i] = second.astype(jnp.bfloat16)
+        above = [t[2 * STEPS:] for t in turned]
+
+    def first_conv(pp, carry):
+        def slab(ref, k):
+            return ref[pp, k:k + ACT_ROWS].reshape(ACT_ROWS * W, LANES)
+
+        lhs = jnp.concatenate(
+            [slab(e01, 0), slab(e01, 1), slab(e01, 2), slab(e2, 0), slab(e2, 2)], axis=1)
+        total = jnp.dot(lhs, w1_ref[...], preferred_element_type=jnp.float32)
+        for i in range(ACT_ROWS):
+            row = R * rows - 1 + i
+            row_in = (row >= 0) & (row < R * ROWS)
             for half in range(2):
                 p = 2 * pp + half
-                cols = slice(half * C, (half + 1) * C)
-                v = total[:, cols] + b1_ref[...]
-                v = v / (1.0 + jnp.exp(-v))
                 keep = row_in & (start - 2 + p >= 0)
-                act[pp, 8:168, cols] = jnp.where(keep, v, 0.0)
-                for e in range(3):
-                    patches[p, at[0], e * C:(e + 1) * C] = (
-                        act[pp, 7 + e:167 + e, cols].astype(jnp.bfloat16))
+                scale = jnp.where(keep, jnp.float32(0.5), jnp.float32(0.0))
+                v = total[W * i:W * (i + 1), half * C:(half + 1) * C] + b1_ref[...]
+                h = v * scale
+                h = h + h * jnp.tanh(h)
+                patches[p, i] = with_edges(h).astype(jnp.bfloat16)
         return carry
 
-    lax.fori_loop(0, ACT_ROWS, first_rows, 0)
+    lax.fori_loop(0, 3, first_conv, 0)
     fetch.wait()
 
     def lhs_of(p):
         return jnp.concatenate(
-            [patches[p, W * b:W * b + SLAB, :] for b in range(3)], axis=1)
+            [patches[p, b:b + R, STEPS * e:STEPS * e + W].reshape(SLAB, C)
+             for b in range(3) for e in range(3)], axis=1)
+
+    def finish(slot, value, live):
+        for y in range(R):
+            for t in range(3):
+                cols = slice(t * LANES, (t + 1) * LANES)
+                for v in range(PHASES):
+                    at = y * W + v * STEPS
+                    natural[t, pl.ds(y * W + v, STEPS, stride=PHASES), :] = value[at:at + STEPS, cols]
+        for t in range(3):
+            cols = slice(t * LANES, (t + 1) * LANES)
+            done = natural[t] + b2_ref[:, cols]
+            if live is not None:
+                done = jnp.where(live, done, 0.0)
+            outs[slot, :, cols] = done.astype(jnp.bfloat16)
 
     def pair(n0, carry):
         @pl.when(own > n0)
@@ -149,11 +166,10 @@
             t = jnp.dot(
                 lhs_of(n0 + 2), jnp.concatenate([w2[2], w2[1]], axis=1),
                 preferred_element_type=jnp.float32)
-            a0 += t[:, :C]
+            finish(n0, a0 + t[:, :C], None)
             a1 += t[:, C:]
             a1 += jnp.dot(lhs_of(n0 + 3), w2[2], preferred_element_type=jnp.float32)
-            outs[n0] = (a0 + b2_ref[...]).astype(jnp.bfloat16)
-            outs[n0 + 1] = jnp.where(own > n0 + 1, a1 + b2_ref[...], 0.0).astype(jnp.bfloat16)
+            finish(n0 + 1, a1, own > n0 + 1)
 
         @pl.when(own <= n0)
         def _():
@@ -181,16 +197,15 @@
         out_shape=jax.ShapeDtypeStruct((FCAP, SLAB, C), jnp.bfloat16),
         scratch_shapes=[
             pltpu.VMEM((3, K2, C), jnp.bfloat16),
-            pltpu.VMEM((2, 176, LANES), jnp.float32),
-            pltpu.VMEM((3, LAT_ROWS * W, LANES), jnp.bfloat16),
-            pltpu.VMEM((3, LAT_ROWS * W, LANES), jnp.bfloat16),
-            pltpu.VMEM((3, 176, 2 * C), jnp.float32),
-            pltpu.VMEM((ACT_FRAMES, ACT_ROWS * W, 3 * C), jnp.bfloat16),
+            pltpu.VMEM((3, LAT_ROWS, W, LANES), jnp.bfloat16),
+            pltpu.VMEM((3, LAT_ROWS, W, LANES), jnp.bfloat16),
+            pltpu.VMEM((ACT_FRAMES, ACT_ROWS, WIDE, C), jnp.bfloat16),
+            pltpu.VMEM((3, SLAB, LANES), jnp.float32),
             pltpu.VMEM((FCAP, SLAB, C), jnp.bfloat16),
             pltpu.SemaphoreType.DMA,
             pltpu.SemaphoreType.DMA((2,)),
         ],
-        compiler_params=pltpu.CompilerParams(vmem_limit_bytes=56 * 1024 * 1024),
+        compiler_params=pltpu.CompilerParams(vmem_limit_bytes=36 * 1024 * 1024),
         name="two_convs",
     )(counts, got, w1, b1, b2, w2)
 
@@ -206,7 +221,7 @@
 
 
 def per_device(latents, token_cell, frame_counts, in_kernel, in_bias, mid_kernel, mid_bias):
-    windows = sort_tokens(frame_counts, token_cell.reshape(1, TOK), latents.T)
+    windows = sort_tokens(frame_counts, token_cell, latents.T)
     by_band = lax.all_to_all(windows, "band", split_axis=0, concat_axis=0, tiled=True)
     edged = jnp.pad(by_band, ((1, 1), (0, 0), (0, 0)))
     spread = jnp.stack([edged[k:k + 15:2] for k in range(4)], axis=1)

time: 66.5 us -> 63 us (0.947)
  the two profiles are of different devices: /device:TPU:4 before, /device:TPU:66 now
where the time goes in v2:
time: 63 us; the launch traced here: 62.2 us
  Pallas kernels  33.2 us (53%)
  starting transfers between devices  12 us (19%)
  waiting for transfers between devices  11.3 us (18%)
  local copies, waits for them, and re-layouts  4.47 us (7%)
  other arithmetic  1.08 us (2%)
    pallas_call x1, Pallas kernels, convs(): pl.pallas_call(conv_kernel, in_specs=[pl.BlockSpec(memory_space=pltpu.SME...  31.2 us
    all_to_all x1, waiting for transfers between devices, per_device(): lax.all_to_all(spread, 'rows', split_axis=0, concat_axis=0, tiled=True)  7.67 us
    all_to_all x1, starting transfers between devices, per_device(): lax.all_to_all(windows, 'band', split_axis=0, concat_axis=0, tiled=True)  7.42 us
    all_to_all x1, starting transfers between devices, per_device(): lax.all_to_all(spread, 'rows', split_axis=0, concat_axis=0, tiled=True)  4.6 us
    unnamed x9, local copies, waits for them, and re-layouts  4.28 us
    all_to_all x1, waiting for transfers between devices, per_device(): lax.all_to_all(windows, 'band', split_axis=0, concat_axis=0, tiled=True)  3.67 us
    pallas_call x1, Pallas kernels, sort_tokens(): pl.pallas_call(sort_kernel, in_specs=[pl.BlockSpec(memory_space=pltpu.SME...  2 us
  transfers between devices with their start and end apart: 2, of which 2 were waited for; matrix products, arithmetic and copies ran while one was open for 2% of the time, Pallas kernels for 0%

profile of v2, /device:TPU:66, one launch (start us, length us, event | category | flops | bytes accessed | tf_op | source)
XLA Modules:
  0.0 62.2 jit_solution(5728679404485366544)
XLA Ops:
  0.0 2.0 %sort_tokens.1 = bf16[16,40,128]{2,1,0:T(8,128)(2,1)} custom-call(s32[16]{0:T(128)} %counts.3, s32[840]{0:T(1024)} %cell_ref.1, bf16[16,840]{1,0:T(8,128)(2,1)} %bitcast.26), custom_call_target="tpu_custom_call" | custom-call | tf_op jit(solution)/shard_map/sort_tokens/pallas_call | solution.py:62
  2.0 7.4 %all-to-all-start = ((bf16[16,40,128]{2,1,0:T(8,128)(2,1)}), bf16[16,40,128]{2,1,0:T(8,128)(2,1)S(1)}, u32[]{:S(2)}, u32[]{:S(2)}) async-start(bf16[16,40,128]{2,1,0:T(8,128)(2,1)} %sort_tokens.1), calls=%async_computation | async-start | bytes 327680 | tf_op jit(solution)/shard_map/all_to_all | solution.py:225
  9.4 1.0 %copy.15 = bf16[3,3,3,16,384]{4,3,0,2,1:T(8,128)(2,1)S(1)} copy(bf16[3,3,3,16,384]{4,3,2,1,0:T(8,128)(2,1)} %param.10) | data formatting | bytes 663552 | tf_op args[3]
  10.4 3.7 %all-to-all-done = bf16[16,40,128]{2,1,0:T(8,128)(2,1)S(1)} async-done(((bf16[16,40,128]{2,1,0:T(8,128)(2,1)}), bf16[16,40,128]{2,1,0:T(8,128)(2,1)S(1)}, u32[]{:S(2)}, u32[]{:S(2)}) %all-to-all-start) | async-done | bytes 163872 | tf_op jit(solution)/shard_map/all_to_all | solution.py:225
  14.1 0.8 %pad_maximum_fusion = bf16[8,4,40,128]{3,2,1,0:T(8,128)(2,1)} fusion(bf16[8,1,40,128]{3,2,1,0:T(8,128)(2,1)S(1)} %get-tuple-element.8, bf16[8,1,40,128]{3,2,1,0:T(8,128)(2,1)S(1)} %get-tuple-element.7, bf16[8,1,40,128]{3,2,1,0:T(8,128)(2,1)S(1)} %get-tuple-element.6, bf16[8,1,40,128]{3,2,1,0:T(8,128)(2,1)S(1)} %get-tuple-element.5), kind=kLoop, calls=%fused_computation.6 | loop fusion | flops 491520 | bytes 655360 | tf_op jit(solution)/shard_map/stack | solution.py:227
  14.9 0.0 copy-start.2
  14.9 0.0 copy-start.3
  14.9 4.6 %all-to-all-start.1 = ((bf16[8,4,40,128]{3,2,1,0:T(8,128)(2,1)}), bf16[8,4,40,128]{3,2,1,0:T(8,128)(2,1)S(1)}, u32[]{:S(2)}, u32[]{:S(2)}) async-start(bf16[8,4,40,128]{3,2,1,0:T(8,128)(2,1)} %pad_maximum_fusion), calls=%async_computation.1 | async-start | bytes 655360 | tf_op jit(solution)/shard_map/all_to_all | solution.py:228
  19.5 0.1 fusion.2
  19.6 0.0 copy-start.1
  19.7 0.0 copy-done.2
  19.7 0.0 copy-done.3
  19.8 0.1 pad.17.clone
  19.8 0.2 maximum_maximum_fusion.w1_ref
  20.1 7.7 %all-to-all-done.1.got_ref = bf16[8,4,40,128]{3,2,1,0:T(8,128)(2,1)S(1)} async-done(((bf16[8,4,40,128]{3,2,1,0:T(8,128)(2,1)}), bf16[8,4,40,128]{3,2,1,0:T(8,128)(2,1)S(1)}, u32[]{:S(2)}, u32[]{:S(2)}) %all-to-all-start.1) | async-done | bytes 327712 | tf_op jit(solution)/shard_map/all_to_all | solution.py:228
  27.7 0.0 copy-done.1
  27.7 0.0 copy-start
  27.7 3.3 %copy-done = bf16[3,3,3,384,384]{4,3,2,1,0:T(8,128)(2,1)S(1)} copy-done((bf16[3,3,3,384,384]{4,3,2,1,0:T(8,128)(2,1)S(1)}, bf16[3,3,3,384,384]{4,3,2,1,0:T(8,128)(2,1)}, u32[]{:S(2)}) %copy-start) | copy-done | bytes 7962648
  31.0 31.2 %two_convs.1 = bf16[4,640,384]{2,1,0:T(8,128)(2,1)} custom-call(s32[16]{0:T(128)S(1)} %copy-done.1, bf16[8,4,40,128]{3,2,1,0:T(8,128)(2,1)S(1)} %all-to-all-done.1.got_ref, bf16[640,768]{1,0:T(8,128)(2,1)S(1)} %maximum_maximum_fusion.w1_ref, f32[1,384]{1,0:T(1,128)S(1)} %reshape.20.b1_ref, f32[1,384]{1,0:T(1,128)S(1)} %reshape.21.b2_ref, ...), custom_call_target="tpu_custom_call" | custom-call | tf_op jit(solution)/shard_map/two_convs/pallas_call | solution.py:190
  (6 shorter events, 0.1 us)
Async XLA Ops:
  2.0 12.1 %all-to-all-start = ((bf16[16,40,128]{2,1,0:T(8,128)(2,1)}), bf16[16,40,128]{2,1,0:T(8,128)(2,1)S(1)}, u32[]{:S(2)}, u32[]{:S(2)}) async-start(bf16[16,40,128]{2,1,0:T(8,128)(2,1)} %sort_tokens.1), calls=%async_computation | async-start | bytes 327680 | tf_op jit(solution)/shard_map/all_to_all | solution.py:225
  14.9 4.8 %copy-start.2 = (f32[384]{0:T(512)S(1)}, f32[384]{0:T(512)}, u32[]{:S(2)}) copy-start(f32[384]{0:T(512)} %param.11) | copy-start | bytes 4612
  14.9 4.8 %copy-start.3 = (f32[384]{0:T(512)S(1)}, f32[384]{0:T(512)}, u32[]{:S(2)}) copy-start(f32[384]{0:T(512)} %param.13) | copy-start | bytes 4612
  14.9 12.8 %all-to-all-start.1 = ((bf16[8,4,40,128]{3,2,1,0:T(8,128)(2,1)}), bf16[8,4,40,128]{3,2,1,0:T(8,128)(2,1)S(1)}, u32[]{:S(2)}, u32[]{:S(2)}) async-start(bf16[8,4,40,128]{3,2,1,0:T(8,128)(2,1)} %pad_maximum_fusion), calls=%async_computation.1 | async-start | bytes 655360 | tf_op jit(solution)/shard_map/all_to_all | solution.py:228
  19.6 8.1 %copy-start.1 = (s32[16]{0:T(128)S(1)}, s32[16]{0:T(128)}, u32[]{:S(2)}) copy-start(s32[16]{0:T(128)} %counts.3) | copy-start | bytes 196
  27.7 3.3 %copy-start = (bf16[3,3,3,384,384]{4,3,2,1,0:T(8,128)(2,1)S(1)}, bf16[3,3,3,384,384]{4,3,2,1,0:T(8,128)(2,1)}, u32[]{:S(2)}) copy-start(bf16[3,3,3,384,384]{4,3,2,1,0:T(8,128)(2,1)} %param.12) | copy-start | bytes 23887876
